TPU v7x, 512 devices: a whole 4x4x16 slice. The times are simulated.
512 devices in a mesh: head: 16 (over z_hi, y, core), seq: 32 (over z_lo, x).
Axes of the slice: x: 4, y: 4, z: 16 (z_hi: 2, z_lo: 8; z = z_hi * 8 + z_lo), core: 2. Of those that a mesh axis runs over, the one named last changes fastest.
Arguments:
- query_rows: bfloat16 [4096, 3072], P(('seq', 'head')), may hold values from -6 to 6
- key_rows: bfloat16 [4096, 3072], P(('seq', 'head')), may hold values from -6 to 6
- value_rows: bfloat16 [4096, 3072], P(('seq', 'head')), may hold values from -6 to 6
- gate_rows: bfloat16 [4096, 3072], P(('seq', 'head')), may hold values from -1 to 1
- step_rates: float32 [4096, 48], P('seq', 'head'), may hold values from 5e-05 to 0.0005
- first_weight: float32 [48, 64, 256], P('head'), may hold values from -0.75 to 0.75
- first_bias: float32 [48, 256], P('head'), may hold values from -3 to 3
- second_weight: float32 [48, 256, 64], P('head'), may hold values from -0.375 to 0.375
- second_bias: float32 [48, 64], P('head'), may hold values from -3 to 3
- norm_gain: float32 [48, 64], P('head'), may hold values from 0.5 to 1.5
- norm_shift: float32 [48, 64], P('head'), may hold values from -3 to 3
Outputs:
- layer_output: bfloat16 [4096, 3072], P(('seq', 'head'))
All inputs are finite; a program needn't handle non-finite values.
Results may differ from a plain program's by a relative error of at most 0.0049.
Values may be sent and summed in bfloat16 or wider, within the bound.
A program may use at most 64 MiB of HBM per device.

v0:
```python
import functools

import jax
import jax.numpy as jnp
from jax import lax
from jax.experimental import pallas as pl
from jax.experimental.pallas import tpu as pltpu
from jax.sharding import PartitionSpec as P

D_HEAD = 64
INNER = 256
MINI = 64
STEPS = 64
LANES = 128
NEAR = 8
CHAIN = 32
HEADS_LOCAL = 3
HEADS_NEAR = 6
WIDE = HEADS_NEAR * D_HEAD
TILES = 24

EPS = 1e-06
ROOT = 0.7978845608028654
CUBE = 0.044715
MESH = pl.DeviceIdType.MESH
F32 = jnp.float32
BF16 = jnp.bfloat16

PACKED = MINI + MINI // 2
HISTORY = 4
SPACING_NS = 700

SEATS = (((4, 17, 26), (15, 24, 5)), ((6, 19, 24), (13, 26, 7)))


def dot(left, right, dims):
    return lax.dot_general(
        left, right, (((dims[0],), (dims[1],)), ((), ())), preferred_element_type=F32
    )


def gelu(values):
    squared = values * values
    tanh_term = jnp.tanh(values * (ROOT + (ROOT * CUBE) * squared))
    return values * (0.5 + 0.5 * tanh_term)


def gelu_and_slope(values):
    squared = values * values
    tanh_term = jnp.tanh(values * (ROOT + (ROOT * CUBE) * squared))
    half = 0.5 + 0.5 * tanh_term
    slope = half + values * (half * (1.0 - tanh_term)) * (ROOT + (3.0 * ROOT * CUBE) * squared)
    return (values * half, slope)


def row_mean(values):
    rows = values.shape[0]
    while rows > 8:
        rows //= 2
        values = values[:rows] + values[rows:]
    return jnp.sum(values, axis=0, keepdims=True) * (1.0 / D_HEAD)


def lanes_left(rows):
    return lax.broadcasted_iota(jnp.int32, (rows, LANES), 1) < D_HEAD


def own_half(stacked):
    return jnp.where(lanes_left(D_HEAD), stacked[:D_HEAD], stacked[D_HEAD:])


def spread_halves(rows):
    left = lanes_left(D_HEAD)
    zero = jnp.zeros_like(rows)
    return jnp.concatenate([jnp.where(left, rows, zero), jnp.where(left, zero, rows)], axis=0)


def seat_of(upper, core, place):
    lower_seat = jnp.where(core == 0, SEATS[0][0][place], SEATS[0][1][place])
    upper_seat = jnp.where(core == 0, SEATS[1][0][place], SEATS[1][1][place])
    return jnp.where(upper == 0, lower_seat, upper_seat)


def kernel(
    query_ref,
    key_ref,
    value_ref,
    gate_ref,
    rates_ref,
    first_ref,
    first_bias_ref,
    second_ref,
    second_bias_ref,
    gain_ref,
    shift_ref,
    out_ref,
    gathered,
    packed,
    rates_out,
    rates_in,
    tokens,
    blocks_out,
    returned,
    relay_out,
    landed,
    kept_rows,
    bd_key,
    turned_query,
    rate_rows,
    target_rows,
    causal,
    halves,
    state_one,
    bias_one,
    state_two,
    second_hist,
    bias_two,
    gain_rows,
    shift_rows,
    slope_ref,
    dual_base,
    dual_act_ref,
    act_ref,
    grad_two_ref,
    grad_one_ref,
    within_ref,
    read_ref,
    attend_ref,
    send_a,
    recv_a,
    send_b,
    recv_b,
    send_r,
    recv_r,
    send_c,
    recv_c,
    send_d,
    recv_d,
):
    head = lax.axis_index("head")
    seq = lax.axis_index("seq")
    core = lax.rem(head, 2)
    upper = head // NEAR
    near = lax.rem(head, NEAR)
    own_mini = 2 * seq + upper
    seats = [seat_of(upper, core, place) for place in range(HEADS_LOCAL)]
    seated = jnp.logical_or(seq == seats[0], jnp.logical_or(seq == seats[1], seq == seats[2]))
    my_place = jnp.where(seq == seats[1], 1, 0) + jnp.where(seq == seats[2], 2, 0)
    my_slot = HEADS_LOCAL * core + my_place
    my_near = head // 2
    own_source = jnp.logical_and(seated, near == my_near)

    targets = [
        (
            2 * near + slot // HEADS_LOCAL,
            seat_of(near // 4, slot // HEADS_LOCAL, slot % HEADS_LOCAL),
        )
        for slot in range(HEADS_NEAR)
    ]

    def other(device):
        return jnp.logical_or(device[0] != head, device[1] != seq)

    def neighbour(step):
        return lax.rem(near + step, NEAR)

    barrier = pltpu.get_barrier_semaphore()

    def greet(device):
        pl.semaphore_signal(barrier, inc=1, device_id=device, device_id_type=MESH)

    @pl.when(seated)
    def _():
        @pl.loop(0, STEPS)
        def _(mini):
            device = (lax.rem(mini, 2) * NEAR + my_near, mini // 2)

            @pl.when(other(device))
            def _():
                greet(device)

        @pl.loop(1, CHAIN)
        def _(step):
            greet((head, lax.rem(seq + step, CHAIN)))

    for device in targets:

        @pl.when(other(device))
        def _():
            greet(device)

    @pl.loop(1, NEAR)
    def _(step):
        greet((upper * NEAR + neighbour(step), seq))

    left_lanes = lanes_left(MINI)
    for place in range(HEADS_LOCAL):
        row = jnp.broadcast_to(rates_ref[place : place + 1], (8, LANES))
        turned_row = pltpu.roll(row, D_HEAD, 1)
        rates_out[place, 0] = jnp.where(left_lanes[:8], row, turned_row)
        rates_out[place, 1] = jnp.where(left_lanes[:8], turned_row, row)

    expected = NEAR - 1 + HEADS_NEAR + HEADS_LOCAL
    expected = expected + jnp.where(seated, STEPS - 1, 0) - jnp.where(own_source, 2, 0)
    pl.semaphore_wait(barrier, expected)

    sources = (query_ref, key_ref, value_ref)

    def wide(index):
        return pl.ds(pl.multiple_of(index * WIDE, LANES), WIDE)

    def rows_of(index):
        return pl.ds(pl.multiple_of(index * 8, 8), 8)

    def exchange_copy(array, step):
        target = neighbour(step)
        return pltpu.make_async_remote_copy(
            src_ref=sources[array].at[:, wide(target)],
            dst_ref=gathered.at[array, rows_of(near)],
            send_sem=send_a.at[array],
            recv_sem=recv_a.at[array],
            device_id=(upper * NEAR + target, seq),
            device_id_type=MESH,
        )

    def own_exchange(array):
        return pltpu.make_async_copy(
            sources[array].at[:, wide(near)], gathered.at[array, rows_of(near)], recv_a.at[array]
        )

    @pl.loop(1, NEAR)
    def _(step):
        for array in range(3):
            exchange_copy(array, step).start()

    for array in range(3):
        own_exchange(array).start()

    def rates_copy(place):
        return pltpu.make_async_remote_copy(
            src_ref=rates_out.at[place],
            dst_ref=rates_in.at[pl.ds(2 * seq, 2)],
            send_sem=send_r.at[place],
            recv_sem=recv_r.at[seq],
            device_id=(head, seats[place]),
            device_id_type=MESH,
        )

    for place in range(HEADS_LOCAL):

        @pl.when(seq != seats[place])
        def _():
            rates_copy(place).start()

    for array in range(3):
        pltpu.make_async_remote_copy(
            src_ref=gathered.at[array],
            dst_ref=gathered.at[array],
            send_sem=send_a.at[array],
            recv_sem=recv_a.at[array],
            device_id=(upper * NEAR + neighbour(1), seq),
            device_id_type=MESH,
        ).wait_recv()

    def relay_copy(slot):
        return pltpu.make_async_remote_copy(
            src_ref=packed.at[slot],
            dst_ref=tokens.at[own_mini],
            send_sem=send_b.at[slot],
            recv_sem=recv_b.at[own_mini],
            device_id=targets[slot],
            device_id_type=MESH,
        )

    for tile in range(HEADS_NEAR // 2):
        columns = slice(tile * LANES, (tile + 1) * LANES)
        queries, keys, values = [gathered[array, :, columns].astype(F32) for array in range(3)]
        queries_turned, keys_turned, values_turned = [
            pltpu.roll(rows, D_HEAD, 1) for rows in (queries, keys, values)
        ]
        first_keys = jnp.where(left_lanes, keys, values_turned)
        second_keys = jnp.where(left_lanes, keys_turned, values)
        half = MINI // 2
        first_queries = jnp.where(left_lanes[:half], queries[:half], queries_turned[half:])
        second_queries = jnp.where(left_lanes[:half], queries_turned[:half], queries[half:])
        packed[2 * tile, :MINI] = first_keys.astype(BF16)
        packed[2 * tile, MINI:] = first_queries.astype(BF16)
        packed[2 * tile + 1, :MINI] = second_keys.astype(BF16)
        packed[2 * tile + 1, MINI:] = second_queries.astype(BF16)

    pl.delay(jnp.minimum(own_mini, STEPS - 1 - own_mini) * SPACING_NS)

    for slot in range(HEADS_NEAR):

        @pl.when(other(targets[slot]))
        def _():
            relay_copy(slot).start()

    @pl.when(seated)
    def _():
        @pl.when(own_source)
        def _():
            tokens[own_mini] = packed[my_slot]

        rates_in[pl.ds(2 * seq, 2)] = rates_out[my_place]

        row = lax.broadcasted_iota(jnp.int32, (LANES, LANES), 0)
        col = lax.broadcasted_iota(jnp.int32, (LANES, LANES), 1)
        ahead = jnp.logical_and(jnp.logical_and(row < 64, col < 64), row <= col)
        back = jnp.logical_and(jnp.logical_and(row >= 64, col >= 64), row >= col)
        causal[...] = jnp.where(jnp.logical_or(ahead, back), 1.0, 0.0)
        halves[...] = jnp.where((row < 64) == (col < 64), 1.0, 0.0)

        first = first_ref[my_place]
        both = jnp.concatenate([first, first], axis=0)
        state_one[...] = both.T
        second = second_ref[my_place]
        second = second - jnp.mean(second, axis=0, keepdims=True)
        doubled = jnp.concatenate([second, second], axis=0)
        state_two[...] = doubled.T
        second_hist[0] = doubled.astype(BF16)

        def spread_column(row_values, length):
            return jnp.broadcast_to(row_values, (LANES, length)).T

        bias_one[...] = spread_column(first_bias_ref[pl.ds(my_place, 1), :], INNER)
        second_bias = second_bias_ref[pl.ds(my_place, 1), :]
        second_bias = second_bias - jnp.mean(second_bias, axis=1, keepdims=True)
        bias_two[0] = spread_column(second_bias, D_HEAD)
        gain_rows[...] = spread_column(gain_ref[pl.ds(my_place, 1), :], D_HEAD)
        shift_rows[...] = spread_column(shift_ref[pl.ds(my_place, 1), :], D_HEAD)

        def await_step(step):
            for mini in (step, STEPS - 1 - step):

                @pl.when(jnp.logical_not(jnp.logical_and(own_source, mini == own_mini)))
                def _():
                    pltpu.make_async_remote_copy(
                        src_ref=packed.at[0],
                        dst_ref=tokens.at[mini],
                        send_sem=send_b.at[0],
                        recv_sem=recv_b.at[mini],
                        device_id=(lax.rem(mini, 2) * NEAR + my_near, mini // 2),
                        device_id_type=MESH,
                    ).wait_recv()

        def await_rates(block):
            @pl.when(block != seq)
            def _():
                pltpu.make_async_remote_copy(
                    src_ref=rates_out.at[0],
                    dst_ref=rates_in.at[pl.ds(2 * block, 2)],
                    send_sem=send_r.at[0],
                    recv_sem=recv_r.at[block],
                    device_id=(head, block),
                    device_id_type=MESH,
                ).wait_recv()

        def load_step(step):
            back = STEPS - 1 - step
            kv_f = tokens[step, :MINI]
            kv_b = tokens[back, :MINI]
            left = lanes_left(MINI)
            keys_back = pltpu.roll(kv_b.astype(F32), D_HEAD, 1)
            keys_bd = jnp.concatenate(
                [jnp.where(left, kv_f.astype(F32), 0.0), jnp.where(left, 0.0, keys_back)], axis=0
            ).astype(BF16)
            pieces = []
            for mini in (step, back):
                pair = tokens[mini, MINI:].astype(F32)
                pieces += [pair, pltpu.roll(pair, D_HEAD, 1)]
            kv_turned = jnp.concatenate([kv_f, kv_b], axis=0).T.astype(F32)
            queries = jnp.concatenate(pieces, axis=0).astype(BF16).T.astype(F32)[:D_HEAD]
            target = kv_turned[D_HEAD:] - kv_turned[:D_HEAD]
            rate = jnp.where(left[:8], rates_in[step], rates_in[back])
            keys_turned = spread_halves(kv_turned[:D_HEAD]).astype(BF16)
            queries_turned = spread_halves(queries).astype(BF16)
            return (keys_bd, keys_turned, queries_turned, target, rate)

        def store_step(loaded):
            bd_key[...] = loaded[0]
            turned_query[...] = loaded[2]
            target_rows[...] = gain_rows[...] * (shift_rows[...] - loaded[3])
            rate_rows[...] = loaded[4]

        def finish(step, dual_two):
            mean = row_mean(dual_two)
            spread = lax.rsqrt(row_mean(dual_two * dual_two) - mean * mean + EPS)
            fitted = gain_rows[...] * ((dual_two - mean) * spread) + shift_rows[...]
            kept_rows[step] = fitted
            total = fitted + pltpu.roll(kept_rows[STEPS - 1 - step], D_HEAD, 1)
            at_left = lax.rem(my_slot, 2) == 0
            total = jnp.concatenate(
                [jnp.where(at_left, total, 0.0), jnp.where(at_left, 0.0, total)], axis=0
            )
            turned = total.astype(BF16).T
            blocks_out[step] = turned[:MINI]
            blocks_out[STEPS - 1 - step] = turned[MINI:]

        def slot_of(step):
            return lax.rem(step, HISTORY)

        def attend_dual(step):
            slot = slot_of(step)
            dual_act = dual_act_ref[lax.rem(step, 2)]
            mask = causal[...]
            read = dot(second_hist[slot], dual_act, (1, 0))
            attend = dot(act_ref[slot].T, dual_act, (1, 0))
            return (own_half(read) + bias_two[slot], (attend * mask + mask).astype(BF16))

        half = INNER // 2
        row_halves = (slice(0, half), slice(half, INNER))

        def widen(grad_one, within, base, bias, ones_bf):
            sums = jnp.concatenate([within, ones_bf], axis=1)
            falls = [dot(grad_one[rows], sums, (1, 0)) for rows in row_halves]
            acts = [
                gelu(base[rows] - fall[:, :LANES]).astype(BF16)
                for rows, fall in zip(row_halves, falls)
            ]
            biases = [bias[rows] - fall[:, LANES:] for rows, fall in zip(row_halves, falls)]
            return (acts, biases)

        def advance(step):
            slot = slot_of(step)
            before = step + HISTORY - 2
            act = act_ref[slot]
            second_turned = second_hist[slot]
            target = target_rows[...]
            gain = gain_rows[...]
            gain_sq = gain * gain
            rate = rate_rows[0:1]
            bias_two_now = bias_two[slot]
            ones_bd = halves[...]
            ones_bf = ones_bd.astype(BF16)
            mask = causal[...]

            pre_two = (
                jnp.where(
                    lanes_left(D_HEAD),
                    dot(second_turned[:D_HEAD], act, (1, 0)),
                    dot(second_turned[D_HEAD:], act, (1, 0)),
                )
                + bias_two_now
            )

            last_read = read_ref[...]
            last_fall = dot(grad_two_ref[slot_of(step + HISTORY - 3)], attend_ref[...], (1, 0))
            dual_acts, biases = widen(
                grad_one_ref[...], within_ref[...], dual_base[...], bias_one[...], ones_bf
            )

            later = jnp.minimum(step + 1, STEPS - 1)
            loaded = load_step(later)
            keys_bd = bd_key[...]
            queries_turned = turned_query[...]
            state_one_now = state_one[...]
            high = state_one_now.astype(BF16)
            low = (state_one_now - high.astype(F32)).astype(BF16)
            reads = jnp.concatenate([loaded[1], queries_turned], axis=1)
            reads = jnp.concatenate([reads, reads], axis=0)
            within_both = dot(
                jnp.concatenate([keys_bd, jnp.zeros_like(keys_bd)], axis=1), reads, (1, 0)
            )
            between = (within_both[:, :LANES] + ones_bd).astype(BF16)
            within = (within_both[:, LANES:] * mask + mask).astype(BF16)

            scaled = gain_sq * pre_two
            mean = row_mean(pre_two)
            sum_scaled = row_mean(scaled)
            sum_square = row_mean(pre_two * pre_two)
            sum_scaled_sq = row_mean(scaled * pre_two)
            sum_target = row_mean(target * pre_two)
            mean_gain = row_mean(gain_sq)
            mean_target = row_mean(target)
            inverse = lax.rsqrt(sum_square - mean * mean + EPS)
            centred_scaled = sum_scaled - mean * mean_gain
            mean_a = inverse * centred_scaled + mean_target
            mean_an = inverse * (
                inverse * (sum_scaled_sq - mean * (sum_scaled + centred_scaled))
                + (sum_target - mean * mean_target)
            )
            weight = inverse * rate
            grad_two = (
                (pre_two - mean) * (inverse * gain_sq - inverse * mean_an) + (target - mean_a)
            ) * weight
            grad_two = grad_two.astype(BF16)
            grad_two_bd = spread_halves(grad_two)
            state_two_now = state_two[...]
            state_two_bf = state_two_now.astype(BF16)
            grads_one = [
                (dot(state_two_bf[rows], grad_two_bd, (1, 0)) * slope_ref[rows, :]).astype(BF16)
                for rows in row_halves
            ]

            finish(jnp.maximum(step - 3, 0), last_read - last_fall)

            state_two_new = state_two_now - dot(act, grad_two_bd.T, (1, 0))
            bias_two_new = bias_two_now - dot(grad_two, ones_bf, (1, 0))
            dual_read, attend = attend_dual(before)
            read_ref[...] = dual_read
            attend_ref[...] = attend

            seen = dot(jnp.concatenate([high, low], axis=1), reads, (1, 0))
            moves = jnp.concatenate([between, keys_bd], axis=1)
            next_slot = slot_of(step + 1)
            for part in range(2):
                rows = row_halves[part]
                fall = dot(grads_one[part], moves, (1, 0))
                state_one[rows, :] = state_one_now[rows] - fall[:, LANES:]
                pre_one = seen[rows, :LANES] + biases[part] - fall[:, :LANES]
                act_next, slope_next = gelu_and_slope(pre_one)
                act_ref[next_slot, rows, :] = act_next.astype(BF16)
                slope_ref[rows, :] = slope_next
                dual_base[rows, :] = seen[rows, LANES:] + biases[part]
                bias_one[rows, :] = biases[part]
                grad_one_ref[rows, :] = grads_one[part]
                dual_act_ref[lax.rem(step + 1, 2), rows, :] = dual_acts[part]

            state_two[...] = state_two_new
            second_hist[next_slot] = state_two_new.astype(BF16).T
            bias_two[next_slot] = bias_two_new
            grad_two_ref[slot] = grad_two
            within_ref[...] = within
            store_step(loaded)

        def emit(step, read, attend):
            finish(step, read - dot(grad_two_ref[slot_of(step)], attend, (1, 0)))
            give_back(step)
            give_back(STEPS - 1 - step)

        def return_copy(mini):
            return pltpu.make_async_remote_copy(
                src_ref=blocks_out.at[mini],
                dst_ref=returned.at[my_slot],
                send_sem=send_c.at[mini],
                recv_sem=recv_c.at[my_slot],
                device_id=(lax.rem(mini, 2) * NEAR + my_near, mini // 2),
                device_id_type=MESH,
            )

        def is_own(mini):
            return jnp.logical_and(own_source, mini == own_mini)

        def give_back(mini):
            @pl.when(jnp.logical_not(is_own(mini)))
            def _():
                return_copy(mini).start()

            @pl.when(is_own(mini))
            def _():
                returned[my_slot] = blocks_out[mini]

        await_rates(0)
        await_rates(CHAIN - 1)
        await_step(0)
        begun = load_step(0)
        store_step(begun)
        high = state_one[...].astype(BF16)
        low = (state_one[...] - high.astype(F32)).astype(BF16)
        act, slope = gelu_and_slope(
            dot(high, begun[1], (1, 0)) + dot(low, begun[1], (1, 0)) + bias_one[...]
        )
        act_ref[0] = act.astype(BF16)
        slope_ref[...] = slope
        grad_one_ref[...] = jnp.zeros_like(grad_one_ref)
        within_ref[...] = jnp.zeros_like(within_ref)

        @pl.loop(0, STEPS)
        def _(step):
            later = step + 1

            @pl.when(later < STEPS // 2)
            def _():
                await_step(later)

                @pl.when(lax.rem(later, 2) == 0)
                def _():
                    await_rates(later // 2)
                    await_rates(CHAIN - 1 - later // 2)

            advance(step)
            done = step - 3

            @pl.when(done >= STEPS // 2)
            def _():
                give_back(done)
                give_back(STEPS - 1 - done)

        last = STEPS - 1
        emit(last - 2, read_ref[...], attend_ref[...])
        dual_acts, _ = widen(
            grad_one_ref[...],
            within_ref[...],
            dual_base[...],
            bias_one[...],
            halves[...].astype(BF16),
        )
        for part in range(2):
            dual_act_ref[last % 2, row_halves[part], :] = dual_acts[part]
        for step in (last - 1, last):
            emit(step, *attend_dual(step))

    for slot in range(HEADS_NEAR):

        @pl.when(other(targets[slot]))
        def _():
            pltpu.make_async_remote_copy(
                src_ref=blocks_out.at[0],
                dst_ref=returned.at[slot],
                send_sem=send_c.at[0],
                recv_sem=recv_c.at[slot],
                device_id=targets[slot],
                device_id_type=MESH,
            ).wait_recv()

    for tile in range(HEADS_NEAR // 2):
        columns = slice(tile * LANES, (tile + 1) * LANES)
        relay_out[:, columns] = jnp.where(left_lanes, returned[2 * tile], returned[2 * tile + 1])

    def spread_copy(step):
        target = neighbour(step)
        return pltpu.make_async_remote_copy(
            src_ref=relay_out.at[rows_of(target)],
            dst_ref=landed.at[:, wide(near)],
            send_sem=send_d.at[0],
            recv_sem=recv_d.at[0],
            device_id=(upper * NEAR + target, seq),
            device_id_type=MESH,
        )

    @pl.loop(1, NEAR)
    def _(step):
        spread_copy(step).start()

    pltpu.make_async_copy(
        relay_out.at[rows_of(near)], landed.at[:, wide(near)], recv_d.at[0]
    ).start()
    pltpu.make_async_remote_copy(
        src_ref=landed,
        dst_ref=landed,
        send_sem=send_d.at[0],
        recv_sem=recv_d.at[0],
        device_id=(upper * NEAR + neighbour(1), seq),
        device_id_type=MESH,
    ).wait_recv()

    for tile in range(TILES):
        columns = slice(tile * LANES, (tile + 1) * LANES)
        out_ref[:, columns] = (
            gate_ref[:, columns].astype(F32) * landed[:, columns].astype(F32)
        ).astype(BF16)

    sent = pl.ds(0, (NEAR - 1) * WIDE)
    for array in range(3):
        pltpu.make_async_remote_copy(
            src_ref=sources[array].at[:, sent],
            dst_ref=sources[array].at[:, sent],
            send_sem=send_a.at[array],
            recv_sem=recv_a.at[array],
            device_id=(upper * NEAR + neighbour(1), seq),
            device_id_type=MESH,
        ).wait_send()
    pltpu.make_async_remote_copy(
        src_ref=relay_out.at[pl.ds(0, 8 * (NEAR - 1))],
        dst_ref=relay_out.at[pl.ds(0, 8 * (NEAR - 1))],
        send_sem=send_d.at[0],
        recv_sem=recv_d.at[0],
        device_id=(upper * NEAR + neighbour(1), seq),
        device_id_type=MESH,
    ).wait_send()

    for place in range(HEADS_LOCAL):

        @pl.when(seq != seats[place])
        def _():
            rates_copy(place).wait_send()

    for slot in range(HEADS_NEAR):

        @pl.when(other(targets[slot]))
        def _():
            relay_copy(slot).wait_send()

    @pl.when(seated)
    def _():
        @pl.loop(0, STEPS)
        def _(mini):
            device = (lax.rem(mini, 2) * NEAR + my_near, mini // 2)

            @pl.when(other(device))
            def _():
                pltpu.make_async_remote_copy(
                    src_ref=blocks_out.at[mini],
                    dst_ref=returned.at[my_slot],
                    send_sem=send_c.at[mini],
                    recv_sem=recv_c.at[my_slot],
                    device_id=device,
                    device_id_type=MESH,
                ).wait_send()


def local(*arrays):
    arrays = list(arrays)
    arrays[4] = arrays[4].T
    arrays[7] = jnp.swapaxes(arrays[7], 1, 2)
    vmem = pl.BlockSpec(memory_space=pltpu.VMEM)
    dma = pltpu.SemaphoreType.DMA
    return pl.pallas_call(
        kernel,
        out_shape=jax.ShapeDtypeStruct((8, TILES * LANES), BF16),
        in_specs=[vmem] * len(arrays),
        out_specs=vmem,
        scratch_shapes=[
            pltpu.VMEM((3, MINI, WIDE), BF16),
            pltpu.VMEM((HEADS_NEAR, PACKED, LANES), BF16),
            pltpu.VMEM((HEADS_LOCAL, 2, 8, LANES), F32),
            pltpu.VMEM((STEPS, 8, LANES), F32),
            pltpu.VMEM((STEPS, PACKED, LANES), BF16),
            pltpu.VMEM((STEPS, MINI, LANES), BF16),
            pltpu.VMEM((HEADS_NEAR, MINI, LANES), BF16),
            pltpu.VMEM((MINI, WIDE), BF16),
            pltpu.VMEM((8, TILES * LANES), BF16),
            pltpu.VMEM((STEPS, D_HEAD, LANES), F32),
            pltpu.VMEM((LANES, LANES), BF16),
            pltpu.VMEM((LANES, LANES), BF16),
            pltpu.VMEM((8, LANES), F32),
            pltpu.VMEM((D_HEAD, LANES), F32),
            pltpu.VMEM((LANES, LANES), F32),
            pltpu.VMEM((LANES, LANES), F32),
            pltpu.VMEM((INNER, LANES), F32),
            pltpu.VMEM((INNER, LANES), F32),
            pltpu.VMEM((INNER, LANES), F32),
            pltpu.VMEM((HISTORY, LANES, INNER), BF16),
            pltpu.VMEM((HISTORY, D_HEAD, LANES), F32),
            pltpu.VMEM((D_HEAD, LANES), F32),
            pltpu.VMEM((D_HEAD, LANES), F32),
            pltpu.VMEM((INNER, LANES), F32),
            pltpu.VMEM((INNER, LANES), F32),
            pltpu.VMEM((2, INNER, LANES), BF16),
            pltpu.VMEM((HISTORY, INNER, LANES), BF16),
            pltpu.VMEM((HISTORY, D_HEAD, LANES), BF16),
            pltpu.VMEM((INNER, LANES), BF16),
            pltpu.VMEM((LANES, LANES), BF16),
            pltpu.VMEM((D_HEAD, LANES), F32),
            pltpu.VMEM((LANES, LANES), BF16),
            dma((3,)),
            dma((3,)),
            dma((HEADS_NEAR,)),
            dma((STEPS,)),
            dma((HEADS_LOCAL,)),
            dma((CHAIN,)),
            dma((STEPS,)),
            dma((HEADS_NEAR,)),
            dma((1,)),
            dma((1,)),
        ],
        compiler_params=pltpu.CompilerParams(collective_id=0, has_side_effects=True),
    )(*arrays)


def solution(mesh):
    rows = P(("seq", "head"), None)
    in_specs = (
        rows,
        rows,
        rows,
        rows,
        P("seq", "head"),
        P("head", None, None),
        P("head", None),
        P("head", None, None),
        P("head", None),
        P("head", None),
        P("head", None),
    )
    return jax.shard_map(local, mesh=mesh, in_specs=in_specs, out_specs=rows, check_vma=False)
```

profile of v0, /device:TPU:1, one launch (start us, length us, event | category | flops | bytes accessed | tf_op | source)
XLA Modules:
  0.0 96.7 jit_solution(13875806604585230326)
XLA Ops:
  0.0 95.2 %shard_map.109 = bf16[8,3072]{1,0:T(8,128)(2,1)} custom-call(bf16[8,3072]{1,0:T(8,128)(2,1)} %query_ref.1, bf16[8,3072]{1,0:T(8,128)(2,1)} %key_ref.1, bf16[8,3072]{1,0:T(8,128)(2,1)} %value_ref.1, bf16[8,3072]{1,0:T(8,128)(2,1)} %gate_ref.1, f32[3,128]{1,0:T(4,128)} %bitcast.3, f32[3,64,256]{2,1,0:T(8,128)} %first_ref.1, f32[3,256]{1,0:T(4,128)} %first_bias_ref.1, ...), custom_call_target="tpu_custom_call" | custom-call | tf_op jit(solution)/shard_map/pallas_call | solution.py:709
  95.2 1.4 %copy.13 = bf16[8,3072]{1,0:T(8,128)(2,1)} copy(bf16[8,3072]{1,0:T(8,128)(2,1)} %shard_map.109) | data formatting | bytes 98304
where the time goes:
time: 96.8 us; the launch traced here: 96.7 us
  Pallas kernels  95.2 us (98%)
  local copies, waits for them, and re-layouts  1.42 us (1%)
    pallas_call x1, Pallas kernels, local(): pl.pallas_call(kernel, out_shape=jax.ShapeDtypeStruct((8, TILES * LANES),...  95.2 us

commit v1 on v0

--- a/solution.py
+++ b/solution.py
@@ -30,7 +30,7 @@
 HISTORY = 4
 SPACING_NS = 700
 
-SEATS = (((4, 17, 26), (15, 24, 5)), ((6, 19, 24), (13, 26, 7)))
+SEATS = (((1, 7, 12), (2, 4, 15)), ((29, 26, 16), (30, 25, 19)))
 
 
 def dot(left, right, dims):
@@ -85,6 +85,15 @@
     query_ref,
     key_ref,
     value_ref,
+    gate_far,
+    rates_far,
+    first_far,
+    first_bias_far,
+    second_far,
+    second_bias_far,
+    gain_far,
+    shift_far,
+    out_ref,
     gate_ref,
     rates_ref,
     first_ref,
@@ -93,7 +102,6 @@
     second_bias_ref,
     gain_ref,
     shift_ref,
-    out_ref,
     gathered,
     packed,
     rates_out,
@@ -126,6 +134,7 @@
     within_ref,
     read_ref,
     attend_ref,
+    load_sem,
     send_a,
     recv_a,
     send_b,
@@ -137,6 +146,24 @@
     send_d,
     recv_d,
 ):
+    fetches = [
+        pltpu.make_async_copy(far, here, load_sem.at[place])
+        for place, (far, here) in enumerate(
+            (
+                (rates_far, rates_ref),
+                (gate_far, gate_ref),
+                (first_far, first_ref),
+                (first_bias_far, first_bias_ref),
+                (second_far, second_ref),
+                (second_bias_far, second_bias_ref),
+                (gain_far, gain_ref),
+                (shift_far, shift_ref),
+            )
+        )
+    ]
+    for fetch in fetches:
+        fetch.start()
+
     head = lax.axis_index("head")
     seq = lax.axis_index("seq")
     core = lax.rem(head, 2)
@@ -193,6 +220,7 @@
     def _(step):
         greet((upper * NEAR + neighbour(step), seq))
 
+    fetches[0].wait()
     left_lanes = lanes_left(MINI)
     for place in range(HEADS_LOCAL):
         row = jnp.broadcast_to(rates_ref[place : place + 1], (8, LANES))
@@ -288,13 +316,17 @@
         packed[2 * tile + 1, :MINI] = second_keys.astype(BF16)
         packed[2 * tile + 1, MINI:] = second_queries.astype(BF16)
 
-    pl.delay(jnp.minimum(own_mini, STEPS - 1 - own_mini) * SPACING_NS)
+    late = jnp.minimum(own_mini, STEPS - 1 - own_mini)
+    pl.delay(jnp.where(seated, 0, late) * SPACING_NS)
 
     for slot in range(HEADS_NEAR):
 
         @pl.when(other(targets[slot]))
         def _():
             relay_copy(slot).start()
+
+    for fetch in fetches[1:]:
+        fetch.wait()
 
     @pl.when(seated)
     def _():
@@ -709,9 +741,10 @@
     return pl.pallas_call(
         kernel,
         out_shape=jax.ShapeDtypeStruct((8, TILES * LANES), BF16),
-        in_specs=[vmem] * len(arrays),
+        in_specs=[pl.BlockSpec(memory_space=pl.ANY)] * len(arrays),
         out_specs=vmem,
         scratch_shapes=[
+            *[pltpu.VMEM(array.shape, array.dtype) for array in arrays[3:]],
             pltpu.VMEM((3, MINI, WIDE), BF16),
             pltpu.VMEM((HEADS_NEAR, PACKED, LANES), BF16),
             pltpu.VMEM((HEADS_LOCAL, 2, 8, LANES), F32),
@@ -744,6 +777,7 @@
             pltpu.VMEM((LANES, LANES), BF16),
             pltpu.VMEM((D_HEAD, LANES), F32),
             pltpu.VMEM((LANES, LANES), BF16),
+            dma((8,)),
             dma((3,)),
             dma((3,)),
             dma((HEADS_NEAR,)),

time: 96.8 us -> 90.6 us (0.936)
  Pallas kernels: 95.2 us -> 89 us
    pallas_call x1, Pallas kernels: 95.2 us -> 89 us  [local(): pl.pallas_call(kernel, out_shape=jax.ShapeDtypeStruct((8, TILES * LANES),...]
where the time goes in v1:
time: 90.6 us; the launch traced here: 90.4 us
  Pallas kernels  89 us (98%)
  local copies, waits for them, and re-layouts  1.42 us (2%)
    pallas_call x1, Pallas kernels, local(): pl.pallas_call(kernel, out_shape=jax.ShapeDtypeStruct((8, TILES * LANES),...  89 us

profile of v1, /device:TPU:1, one launch (start us, length us, event | category | flops | bytes accessed | tf_op | source)
XLA Modules:
  0.0 90.4 jit_solution(7710780349616009978)
XLA Ops:
  0.0 89.0 %shard_map.109 = bf16[8,3072]{1,0:T(8,128)(2,1)} custom-call(bf16[8,3072]{1,0:T(8,128)(2,1)} %query_ref.1, bf16[8,3072]{1,0:T(8,128)(2,1)} %key_ref.1, bf16[8,3072]{1,0:T(8,128)(2,1)} %value_ref.1, bf16[8,3072]{1,0:T(8,128)(2,1)} %gate_far.1, f32[3,128]{1,0:T(4,128)} %bitcast.3, f32[3,64,256]{2,1,0:T(8,128)} %first_far.1, f32[3,256]{1,0:T(4,128)} %first_bias_far.1, ...), custom_call_target="tpu_custom_call" | custom-call | tf_op jit(solution)/shard_map/pallas_call | solution.py:741
  89.0 1.4 %copy.13 = bf16[8,3072]{1,0:T(8,128)(2,1)} copy(bf16[8,3072]{1,0:T(8,128)(2,1)} %shard_map.109) | data formatting | bytes 98304

commit v2 on v1

--- a/solution.py
+++ b/solution.py
@@ -28,7 +28,7 @@
 
 PACKED = MINI + MINI // 2
 HISTORY = 4
-SPACING_NS = 700
+SPACING_NS = 665
 
 SEATS = (((1, 7, 12), (2, 4, 15)), ((29, 26, 16), (30, 25, 19)))
 
@@ -85,7 +85,6 @@
     query_ref,
     key_ref,
     value_ref,
-    gate_far,
     rates_far,
     first_far,
     first_bias_far,
@@ -93,8 +92,7 @@
     second_bias_far,
     gain_far,
     shift_far,
-    out_ref,
-    gate_ref,
+    landed,
     rates_ref,
     first_ref,
     first_bias_ref,
@@ -110,7 +108,6 @@
     blocks_out,
     returned,
     relay_out,
-    landed,
     kept_rows,
     bd_key,
     turned_query,
@@ -151,7 +148,6 @@
         for place, (far, here) in enumerate(
             (
                 (rates_far, rates_ref),
-                (gate_far, gate_ref),
                 (first_far, first_ref),
                 (first_bias_far, first_bias_ref),
                 (second_far, second_ref),
@@ -199,7 +195,8 @@
     @pl.when(seated)
     def _():
         @pl.loop(0, STEPS)
-        def _(mini):
+        def _(turn):
+            mini = jnp.where(lax.rem(turn, 2) == 0, turn // 2, STEPS - 1 - turn // 2)
             device = (lax.rem(mini, 2) * NEAR + my_near, mini // 2)
 
             @pl.when(other(device))
@@ -558,8 +555,6 @@
 
         def emit(step, read, attend):
             finish(step, read - dot(grad_two_ref[slot_of(step)], attend, (1, 0)))
-            give_back(step)
-            give_back(STEPS - 1 - step)
 
         def return_copy(mini):
             return pltpu.make_async_remote_copy(
@@ -620,7 +615,6 @@
                 give_back(STEPS - 1 - done)
 
         last = STEPS - 1
-        emit(last - 2, read_ref[...], attend_ref[...])
         dual_acts, _ = widen(
             grad_one_ref[...],
             within_ref[...],
@@ -628,10 +622,16 @@
             bias_one[...],
             halves[...].astype(BF16),
         )
+        later = attend_dual(last - 1)
+        emit(last - 2, read_ref[...], attend_ref[...])
         for part in range(2):
             dual_act_ref[last % 2, row_halves[part], :] = dual_acts[part]
-        for step in (last - 1, last):
-            emit(step, *attend_dual(step))
+        latest = attend_dual(last)
+        emit(last - 1, *later)
+        emit(last, *latest)
+        for step in (last, last - 1, last - 2):
+            give_back(step)
+            give_back(STEPS - 1 - step)
 
     for slot in range(HEADS_NEAR):
 
@@ -676,12 +676,6 @@
         device_id=(upper * NEAR + neighbour(1), seq),
         device_id_type=MESH,
     ).wait_recv()
-
-    for tile in range(TILES):
-        columns = slice(tile * LANES, (tile + 1) * LANES)
-        out_ref[:, columns] = (
-            gate_ref[:, columns].astype(F32) * landed[:, columns].astype(F32)
-        ).astype(BF16)
 
     sent = pl.ds(0, (NEAR - 1) * WIDE)
     for array in range(3):
@@ -736,13 +730,14 @@
     arrays = list(arrays)
     arrays[4] = arrays[4].T
     arrays[7] = jnp.swapaxes(arrays[7], 1, 2)
-    vmem = pl.BlockSpec(memory_space=pltpu.VMEM)
+    gate = arrays.pop(3)
+    anywhere = pl.BlockSpec(memory_space=pl.ANY)
     dma = pltpu.SemaphoreType.DMA
-    return pl.pallas_call(
+    summed = pl.pallas_call(
         kernel,
         out_shape=jax.ShapeDtypeStruct((8, TILES * LANES), BF16),
-        in_specs=[pl.BlockSpec(memory_space=pl.ANY)] * len(arrays),
-        out_specs=vmem,
+        in_specs=[anywhere] * len(arrays),
+        out_specs=anywhere,
         scratch_shapes=[
             *[pltpu.VMEM(array.shape, array.dtype) for array in arrays[3:]],
             pltpu.VMEM((3, MINI, WIDE), BF16),
@@ -753,7 +748,6 @@
             pltpu.VMEM((STEPS, MINI, LANES), BF16),
             pltpu.VMEM((HEADS_NEAR, MINI, LANES), BF16),
             pltpu.VMEM((MINI, WIDE), BF16),
-            pltpu.VMEM((8, TILES * LANES), BF16),
             pltpu.VMEM((STEPS, D_HEAD, LANES), F32),
             pltpu.VMEM((LANES, LANES), BF16),
             pltpu.VMEM((LANES, LANES), BF16),
@@ -777,7 +771,7 @@
             pltpu.VMEM((LANES, LANES), BF16),
             pltpu.VMEM((D_HEAD, LANES), F32),
             pltpu.VMEM((LANES, LANES), BF16),
-            dma((8,)),
+            dma((7,)),
             dma((3,)),
             dma((3,)),
             dma((HEADS_NEAR,)),
@@ -791,6 +785,7 @@
         ],
         compiler_params=pltpu.CompilerParams(collective_id=0, has_side_effects=True),
     )(*arrays)
+    return (gate.astype(F32) * summed.astype(F32)).astype(BF16)
 
 
 def solution(mesh):

time: 90.6 us -> 89.4 us (0.987)
  other arithmetic: 0 us -> 1.43 us
  local copies, waits for them, and re-layouts: 1.42 us -> 0.01 us
  Pallas kernels: 89 us -> 87.7 us
    convert_element_type x0 -> x1, other arithmetic: none -> 1.43 us  [local(): return (gate.astype(F32) * summed.astype(F32)).astype(BF16)]
    unnamed x1 -> x2, local copies, waits for them, and re-layouts: 1.42 us -> 0.01 us
    pallas_call x1, Pallas kernels: 89 us -> 87.7 us  [local(): pl.pallas_call(kernel, out_shape=jax.ShapeDtypeStruct((8, TILES * LANES),...]
where the time goes in v2:
time: 89.4 us; the launch traced here: 89.2 us
  Pallas kernels  87.7 us (98%)
  other arithmetic  1.43 us (2%)
    pallas_call x1, Pallas kernels, local(): pl.pallas_call(kernel, out_shape=jax.ShapeDtypeStruct((8, TILES * LANES),...  87.7 us

profile of v2, /device:TPU:1, one launch (start us, length us, event | category | flops | bytes accessed | tf_op | source)
XLA Modules:
  0.0 89.2 jit_solution(42028144639358029)
XLA Ops:
  0.0 0.0 copy-start
  0.0 87.7 %shard_map.109 = bf16[8,3072]{1,0:T(8,128)(2,1)} custom-call(bf16[8,3072]{1,0:T(8,128)(2,1)} %query_ref.1, bf16[8,3072]{1,0:T(8,128)(2,1)} %key_ref.1, bf16[8,3072]{1,0:T(8,128)(2,1)} %value_ref.1, f32[3,128]{1,0:T(4,128)} %bitcast.3, f32[3,64,256]{2,1,0:T(8,128)} %first_far.1, f32[3,256]{1,0:T(4,128)} %first_bias_far.1, f32[3,64,256]{2,1,0:T(8,128)} %bitcast.2, ...), custom_call_target="tpu_custom_call" | custom-call | tf_op jit(solution)/shard_map/pallas_call | solution.py:736
  87.7 0.0 copy-done
  87.8 1.4 %multiply_convert_fusion = bf16[8,3072]{1,0:T(8,128)(2,1)} fusion(bf16[8,3072]{1,0:T(8,128)(2,1)} %shard_map.109, bf16[8,3072]{1,0:T(8,128)(2,1)S(1)} %copy-done), kind=kLoop, calls=%fused_computation | loop fusion | flops 98304 | bytes 147456 | tf_op jit(solution)/shard_map/convert_element_type | solution.py:788
Async XLA Ops:
  0.0 87.7 %copy-start = (bf16[8,3072]{1,0:T(8,128)(2,1)S(1)}, bf16[8,3072]{1,0:T(8,128)(2,1)}, u32[]{:S(2)}) copy-start(bf16[8,3072]{1,0:T(8,128)(2,1)} %param.14) | copy-start | bytes 147460

commit v3 on v2

--- a/solution.py
+++ b/solution.py
@@ -28,7 +28,7 @@
 
 PACKED = MINI + MINI // 2
 HISTORY = 4
-SPACING_NS = 665
+SPACING_NS = 640
 
 SEATS = (((1, 7, 12), (2, 4, 15)), ((29, 26, 16), (30, 25, 19)))
 

time: 89.4 us -> 88.6 us (level)
  no operation moved by 1% of the time
where the time goes in v3:
time: 88.6 us; the launch traced here: 88.4 us
  Pallas kernels  87 us (98%)
  other arithmetic  1.43 us (2%)
    pallas_call x1, Pallas kernels, local(): pl.pallas_call(kernel, out_shape=jax.ShapeDtypeStruct((8, TILES * LANES),...  87 us

profile of v3, /device:TPU:1, one launch (start us, length us, event | category | flops | bytes accessed | tf_op | source)
XLA Modules:
  0.0 88.4 jit_solution(809018756130131849)
XLA Ops:
  0.0 0.0 copy-start
  0.0 87.0 %shard_map.109 = bf16[8,3072]{1,0:T(8,128)(2,1)} custom-call(bf16[8,3072]{1,0:T(8,128)(2,1)} %query_ref.1, bf16[8,3072]{1,0:T(8,128)(2,1)} %key_ref.1, bf16[8,3072]{1,0:T(8,128)(2,1)} %value_ref.1, f32[3,128]{1,0:T(4,128)} %bitcast.3, f32[3,64,256]{2,1,0:T(8,128)} %first_far.1, f32[3,256]{1,0:T(4,128)} %first_bias_far.1, f32[3,64,256]{2,1,0:T(8,128)} %bitcast.2, ...), custom_call_target="tpu_custom_call" | custom-call | tf_op jit(solution)/shard_map/pallas_call | solution.py:736
  87.0 0.0 copy-done
  87.0 1.4 %multiply_convert_fusion = bf16[8,3072]{1,0:T(8,128)(2,1)} fusion(bf16[8,3072]{1,0:T(8,128)(2,1)} %shard_map.109, bf16[8,3072]{1,0:T(8,128)(2,1)S(1)} %copy-done), kind=kLoop, calls=%fused_computation | loop fusion | flops 98304 | bytes 147456 | tf_op jit(solution)/shard_map/convert_element_type | solution.py:788
Async XLA Ops:
  0.0 87.0 %copy-start = (bf16[8,3072]{1,0:T(8,128)(2,1)S(1)}, bf16[8,3072]{1,0:T(8,128)(2,1)}, u32[]{:S(2)}) copy-start(bf16[8,3072]{1,0:T(8,128)(2,1)} %param.14) | copy-start | bytes 147460

commit v4 on v3

--- a/solution.py
+++ b/solution.py
@@ -28,7 +28,7 @@
 
 PACKED = MINI + MINI // 2
 HISTORY = 4
-SPACING_NS = 640
+SPACING_NS = 625
 
 SEATS = (((1, 7, 12), (2, 4, 15)), ((29, 26, 16), (30, 25, 19)))
 

time: 88.6 us -> 88.3 us (level)
  no operation moved by 1% of the time
where the time goes in v4:
time: 88.3 us; the launch traced here: 88.1 us
  Pallas kernels  86.7 us (98%)
  other arithmetic  1.43 us (2%)
    pallas_call x1, Pallas kernels, local(): pl.pallas_call(kernel, out_shape=jax.ShapeDtypeStruct((8, TILES * LANES),...  86.7 us

profile of v4, /device:TPU:1, one launch (start us, length us, event | category | flops | bytes accessed | tf_op | source)
XLA Modules:
  0.0 88.1 jit_solution(1410328598365863299)
XLA Ops:
  0.0 0.0 copy-start
  0.0 86.7 %shard_map.109 = bf16[8,3072]{1,0:T(8,128)(2,1)} custom-call(bf16[8,3072]{1,0:T(8,128)(2,1)} %query_ref.1, bf16[8,3072]{1,0:T(8,128)(2,1)} %key_ref.1, bf16[8,3072]{1,0:T(8,128)(2,1)} %value_ref.1, f32[3,128]{1,0:T(4,128)} %bitcast.3, f32[3,64,256]{2,1,0:T(8,128)} %first_far.1, f32[3,256]{1,0:T(4,128)} %first_bias_far.1, f32[3,64,256]{2,1,0:T(8,128)} %bitcast.2, ...), custom_call_target="tpu_custom_call" | custom-call | tf_op jit(solution)/shard_map/pallas_call | solution.py:736
  86.7 0.0 copy-done
  86.7 1.4 %multiply_convert_fusion = bf16[8,3072]{1,0:T(8,128)(2,1)} fusion(bf16[8,3072]{1,0:T(8,128)(2,1)} %shard_map.109, bf16[8,3072]{1,0:T(8,128)(2,1)S(1)} %copy-done), kind=kLoop, calls=%fused_computation | loop fusion | flops 98304 | bytes 147456 | tf_op jit(solution)/shard_map/convert_element_type | solution.py:788
Async XLA Ops:
  0.0 86.7 %copy-start = (bf16[8,3072]{1,0:T(8,128)(2,1)S(1)}, bf16[8,3072]{1,0:T(8,128)(2,1)}, u32[]{:S(2)}) copy-start(bf16[8,3072]{1,0:T(8,128)(2,1)} %param.14) | copy-start | bytes 147460

commit v5 on v4

--- a/solution.py
+++ b/solution.py
@@ -28,7 +28,7 @@
 
 PACKED = MINI + MINI // 2
 HISTORY = 4
-SPACING_NS = 625
+SPACING_NS = 612
 
 SEATS = (((1, 7, 12), (2, 4, 15)), ((29, 26, 16), (30, 25, 19)))
 

time: 88.3 us -> 88 us (level)
  no operation moved by 1% of the time
where the time goes in v5:
time: 88 us; the launch traced here: 87.8 us
  Pallas kernels  86.4 us (98%)
  other arithmetic  1.43 us (2%)
    pallas_call x1, Pallas kernels, local(): pl.pallas_call(kernel, out_shape=jax.ShapeDtypeStruct((8, TILES * LANES),...  86.4 us

profile of v5, /device:TPU:1, one launch (start us, length us, event | category | flops | bytes accessed | tf_op | source)
XLA Modules:
  0.0 87.8 jit_solution(6754831270214771990)
XLA Ops:
  0.0 0.0 copy-start
  0.0 86.4 %shard_map.109 = bf16[8,3072]{1,0:T(8,128)(2,1)} custom-call(bf16[8,3072]{1,0:T(8,128)(2,1)} %query_ref.1, bf16[8,3072]{1,0:T(8,128)(2,1)} %key_ref.1, bf16[8,3072]{1,0:T(8,128)(2,1)} %value_ref.1, f32[3,128]{1,0:T(4,128)} %bitcast.3, f32[3,64,256]{2,1,0:T(8,128)} %first_far.1, f32[3,256]{1,0:T(4,128)} %first_bias_far.1, f32[3,64,256]{2,1,0:T(8,128)} %bitcast.2, ...), custom_call_target="tpu_custom_call" | custom-call | tf_op jit(solution)/shard_map/pallas_call | solution.py:736
  86.4 0.0 copy-done
  86.4 1.4 %multiply_convert_fusion = bf16[8,3072]{1,0:T(8,128)(2,1)} fusion(bf16[8,3072]{1,0:T(8,128)(2,1)} %shard_map.109, bf16[8,3072]{1,0:T(8,128)(2,1)S(1)} %copy-done), kind=kLoop, calls=%fused_computation | loop fusion | flops 98304 | bytes 147456 | tf_op jit(solution)/shard_map/convert_element_type | solution.py:788
Async XLA Ops:
  0.0 86.4 %copy-start = (bf16[8,3072]{1,0:T(8,128)(2,1)S(1)}, bf16[8,3072]{1,0:T(8,128)(2,1)}, u32[]{:S(2)}) copy-start(bf16[8,3072]{1,0:T(8,128)(2,1)} %param.14) | copy-start | bytes 147460

commit v6 on v5

--- a/solution.py
+++ b/solution.py
@@ -213,8 +213,7 @@
         def _():
             greet(device)
 
-    @pl.loop(1, NEAR)
-    def _(step):
+    for step in range(1, NEAR):
         greet((upper * NEAR + neighbour(step), seq))
 
     fetches[0].wait()
@@ -253,8 +252,7 @@
             sources[array].at[:, wide(near)], gathered.at[array, rows_of(near)], recv_a.at[array]
         )
 
-    @pl.loop(1, NEAR)
-    def _(step):
+    for step in range(1, NEAR):
         for array in range(3):
             exchange_copy(array, step).start()
 
@@ -661,8 +659,7 @@
             device_id_type=MESH,
         )
 
-    @pl.loop(1, NEAR)
-    def _(step):
+    for step in range(1, NEAR):
         spread_copy(step).start()
 
     pltpu.make_async_copy(

time: 88 us -> 88 us (level)
  no operation moved by 1% of the time
where the time goes in v6:
time: 88 us; the launch traced here: 87.8 us
  Pallas kernels  86.3 us (98%)
  other arithmetic  1.43 us (2%)
    pallas_call x1, Pallas kernels, local(): pl.pallas_call(kernel, out_shape=jax.ShapeDtypeStruct((8, TILES * LANES),...  86.3 us

profile of v6, /device:TPU:1, one launch (start us, length us, event | category | flops | bytes accessed | tf_op | source)
XLA Modules:
  0.0 87.8 jit_solution(7549804022714922119)
XLA Ops:
  0.0 0.0 copy-start
  0.0 86.3 %shard_map.109 = bf16[8,3072]{1,0:T(8,128)(2,1)} custom-call(bf16[8,3072]{1,0:T(8,128)(2,1)} %query_ref.1, bf16[8,3072]{1,0:T(8,128)(2,1)} %key_ref.1, bf16[8,3072]{1,0:T(8,128)(2,1)} %value_ref.1, f32[3,128]{1,0:T(4,128)} %bitcast.3, f32[3,64,256]{2,1,0:T(8,128)} %first_far.1, f32[3,256]{1,0:T(4,128)} %first_bias_far.1, f32[3,64,256]{2,1,0:T(8,128)} %bitcast.2, ...), custom_call_target="tpu_custom_call" | custom-call | tf_op jit(solution)/shard_map/pallas_call | solution.py:733
  86.3 0.0 copy-done
  86.4 1.4 %multiply_convert_fusion = bf16[8,3072]{1,0:T(8,128)(2,1)} fusion(bf16[8,3072]{1,0:T(8,128)(2,1)} %shard_map.109, bf16[8,3072]{1,0:T(8,128)(2,1)S(1)} %copy-done), kind=kLoop, calls=%fused_computation | loop fusion | flops 98304 | bytes 147456 | tf_op jit(solution)/shard_map/convert_element_type | solution.py:785
Async XLA Ops:
  0.0 86.3 %copy-start = (bf16[8,3072]{1,0:T(8,128)(2,1)S(1)}, bf16[8,3072]{1,0:T(8,128)(2,1)}, u32[]{:S(2)}) copy-start(bf16[8,3072]{1,0:T(8,128)(2,1)} %param.14) | copy-start | bytes 147460
